TPU v7x, 128 devices: a whole 4x4x4 slice. The times are simulated.
128 devices in a mesh: oi: 4 (over z_lo, core), oj: 4 (over y), vir: 8 (over z_hi, x).
Axes of the slice: x: 4, y: 4, z: 4 (z_hi: 2, z_lo: 2; z = z_hi * 2 + z_lo), core: 2. Of those that a mesh axis runs over, the one named last changes fastest.
Arguments:
- amplitudes: float32 [8, 8, 1024, 1024], P('oi', 'oj', 'vir'), may hold values from -6 to 6
- integrals: float32 [8, 8, 1024, 1024], P('oi', 'oj', 'vir'), may hold values from -0.0007324219 to 0.0007324219
- fock_virtual: float32 [1024, 1024], P('vir'), may hold values from -0.1875 to 0.1875
- screening: int32 [4, 4, 8, 8], P('oi', 'oj'), may hold values 0 or 1
Outputs:
- symmetric_residual: float32 [8, 8, 1024, 1024], P('oi', 'oj', 'vir')
Inputs may be any that keep to these rules, and one draw needn't show every extreme that they name: `screening`: entry (p, q, s, t) screens virtual blocks s and t of occupied block pair p, q.
All inputs are finite; a program needn't handle non-finite values.
Results may differ from a plain program's by a relative error of at most 0.00007.
Values sent between devices are 32-bit elements; how exact they have to be, the bound alone decides.
A program may use at most 128 MiB of HBM per device.

v0:
```python
import jax
import jax.numpy as jnp
from jax import lax
from jax.sharding import PartitionSpec as P

BLK = 128


highest = lax.Precision.HIGHEST


def body(amplitudes, integrals, fock_virtual, screening):
    occ = amplitudes.shape[0]
    rows_here = amplitudes.shape[2]
    width = amplitudes.shape[3]
    pairs = occ * occ
    vir_place = lax.axis_index("vir")
    nblocks = rows_here // BLK
    block_rows = lax.dynamic_slice(
        screening[0, 0], (vir_place * nblocks, jnp.int32(0)), (nblocks, width // BLK)
    )
    dense = jnp.repeat(jnp.repeat(block_rows.astype(jnp.float32), BLK, axis=0), BLK, axis=1)
    screened = (amplitudes * dense[None, None]).reshape(pairs, rows_here, width)
    piece = lax.all_gather(integrals, "vir", axis=2, tiled=True)
    count = piece.shape[2]
    flat = piece.reshape(pairs, count, width)
    added = jnp.einsum("pad,pcd->ac", screened, flat, precision=highest)
    gathered = (
        lax.all_gather(fock_virtual, "vir", axis=0, tiled=True),
        lax.all_gather(added, "vir", axis=0, tiled=True),
    )
    whole_sum = lax.psum(gathered[1], ("oi", "oj"))
    dressed = gathered[0] - whole_sum
    second_term = jnp.einsum("pac,bc->pab", screened, dressed, precision=highest)
    columns = lax.dynamic_slice_in_dim(dressed, vir_place * rows_here, rows_here, 1)
    first_term = lax.psum_scatter(
        jnp.einsum("ac,pcb->apb", columns, screened, precision=highest),
        "vir",
        scatter_dimension=0,
        tiled=True,
    )
    residual_here = jnp.transpose(first_term, (1, 0, 2)) + second_term
    residual_turned = lax.all_to_all(residual_here, "vir", split_axis=2, concat_axis=1, tiled=True)
    swapped = jnp.transpose(residual_turned.reshape(occ, occ, width, rows_here), (1, 0, 3, 2))
    sectioned = lax.all_to_all(swapped[None], "oj", split_axis=4, concat_axis=0, tiled=True)
    routed = lax.all_to_all(
        lax.all_to_all(sectioned, "oi", split_axis=0, concat_axis=0, tiled=True),
        "oj",
        split_axis=0,
        concat_axis=0,
        tiled=True,
    )
    mirrored = jnp.transpose(routed, (1, 2, 3, 0, 4)).reshape(occ, occ, rows_here, width)
    return residual_here.reshape(occ, occ, rows_here, width) + mirrored


def solution(mesh):
    placed = (
        P("oi", "oj", "vir", None),
        P("oi", "oj", "vir", None),
        P("vir", None),
        P("oi", "oj", None, None),
    )
    return jax.shard_map(
        body, mesh=mesh, in_specs=placed, out_specs=P("oi", "oj", "vir", None), check_vma=False
    )
```

profile of v0, /device:TPU:24, one launch (start us, length us, event | category | flops | bytes accessed | tf_op | source)
XLA Modules:
  0.0 862.1 jit_solution(6574331192889588102)
XLA Ops:
  8.1 1.9 broadcast_multiply_fusion
  10.0 187.2 %all-gather.6.cloned.1.call-done = f32[2,2,1024,1024]{3,2,1,0:T(8,128)} async-done(((f32[2,2,128,1024]{3,2,1,0:T(8,128)}), f32[2,2,1024,1024]{3,2,1,0:T(8,128)}) %all-gather.6.cloned.1.call-update) | async-done | bytes 16777232 | tf_op jit(solution)/shard_map/all_gather | solution.py:24
  197.2 20.6 %convolution_bitcast_fusion = f32[128,1024]{1,0:T(8,128)} fusion(f32[4,128,1024]{2,1,0:T(8,128)S(1)} %bitcast.41, f32[4,1024,1024]{2,1,0:T(8,128)} %bitcast.45), kind=kOutput, calls=%fused_computation.5 | convolution fusion | flops 6442450944 | bytes 19398656 | tf_op jit(solution)/shard_map/pad,pcd->ac/dot_general | solution.py:27
  218.7 68.7 %all-gather.8.cloned.1.call-done = f32[1024,1024]{1,0:T(8,128)} async-done(((f32[128,1024]{1,0:T(8,128)}), f32[1024,1024]{1,0:T(8,128)}) %all-gather.8.cloned.1.call-update) | async-done | bytes 4194320 | tf_op jit(solution)/shard_map/all_gather | solution.py:30
  287.6 71.4 %all-gather.4.cloned.1.call-done = f32[1024,1024]{1,0:T(8,128)} async-done(((f32[128,1024]{1,0:T(8,128)}), f32[1024,1024]{1,0:T(8,128)}) %all-gather.4.cloned.1.call-update) | async-done | bytes 4194320 | tf_op jit(solution)/shard_map/all_gather | solution.py:29
  359.0 137.2 %all-reduce.2.cloned.1.call-done = f32[1024,1024]{1,0:T(8,128)} async-done(((f32[1024,1024]{1,0:T(8,128)}), f32[1024,1024]{1,0:T(8,128)}) %all-reduce.2.cloned.1.call-update) | async-done | bytes 4194320 | tf_op jit(solution)/shard_map/psum | solution.py:32
  496.2 4.4 sub.3
  500.6 1.9 copy-done
  502.6 16.0 %fusion.4 = f32[1024,4,1024]{2,0,1:T(8,128)} fusion(f32[4,128,1024]{2,1,0:T(8,128)S(1)} %bitcast.42, f32[1024,1024]{1,0:T(8,128)S(1)} %sub.3, s32[]{:T(128)S(6)} %select_n.7), kind=kOutput, calls=%fused_computation.7 | convolution fusion | flops 6442450944 | bytes 19398660 | tf_op jit(solution)/shard_map/ac,pcb->apb/dot_general | solution.py:37
  518.6 195.0 %reduce-scatter.2.cloned.1.call-done = f32[128,4,1024]{2,0,1:T(8,128)} async-done(((f32[1024,4,1024]{2,0,1:T(8,128)}), f32[128,4,1024]{2,0,1:T(8,128)}) %reduce-scatter.2.cloned.1.call-update) | async-done | bytes 2097168 | tf_op jit(solution)/shard_map/reduce_scatter | solution.py:36
  713.7 9.9 %bitcast_add_fusion.1 = f32[4,128,1024]{2,1,0:T(8,128)} fusion(f32[128,4,1024]{2,0,1:T(8,128)} %reduce-scatter.2.cloned.1.call-done, f32[4,128,1024]{2,1,0:T(8,128)S(1)} %bitcast.43, f32[1024,1024]{1,0:T(8,128)} %copy-done), kind=kOutput, calls=%fused_computation.3 | convolution fusion | flops 6442975232 | bytes 10485760 | tf_op jit(solution)/shard_map/pac,bc->pab/dot_general | solution.py:34
  723.6 2.9 copy.10
  726.5 31.7 %all_to_all.43 = f32[4,128,1024]{1,0,2:T(4,128)S(1)} all-to-all(f32[4,128,1024]{1,0,2:T(4,128)} %copy.10), channel_id=1, replica_groups=mesh['oi'=4,'oj'=4,'vir'=8] {'vir'}, dimensions={2} | all-to-all | bytes 4194304 | tf_op jit(solution)/shard_map/all_to_all | solution.py:43
  758.2 1.5 copy.11
  759.7 1.9 copy.12
  761.6 1.6 copy.13
  763.2 26.0 %all_to_all.44 = f32[1,2,2,128,1024]{3,1,2,0,4:T(2,128)S(1)} all-to-all(f32[1,2,2,128,1024]{3,1,2,0,4:T(2,128)S(1)} %copy.13), channel_id=1, replica_groups=mesh['oi'=4,'oj'=4,'vir'=8] {'oj'}, dimensions={4} | all-to-all | bytes 4194304 | tf_op jit(solution)/shard_map/all_to_all | solution.py:45
  789.5 28.9 %all_to_all.45 = f32[4,2,2,128,256]{3,4,1,2,0:T(8,128)} all-to-all(f32[4,2,2,128,256]{3,4,1,2,0:T(8,128)S(1)} %bitcast.49), channel_id=1, replica_groups=mesh['oi'=4,'oj'=4,'vir'=8] {'oi'}, dimensions={0} | all-to-all | bytes 4194304 | tf_op jit(solution)/shard_map/all_to_all | solution.py:47
  818.4 6.6 all-to-all-start.3
  825.0 1.8 copy.16
  826.8 22.5 %all-to-all-done.3 = f32[4,2,2,128,256]{3,4,1,2,0:T(8,128)} async-done(((f32[4,2,2,128,256]{3,4,1,2,0:T(8,128)}), f32[4,2,2,128,256]{3,4,1,2,0:T(8,128)}, u32[]{:S(2)}, u32[]{:S(2)}) %all-to-all-start.3) | async-done | bytes 2097184 | tf_op jit(solution)/shard_map/all_to_all | solution.py:46
  849.3 1.7 copy.15
  851.0 1.7 bitcast_add_fusion
  852.7 2.9 copy.17
  (18 shorter events, 2.8 us)
Async XLA Ops:
  6.5 190.7 %all-gather.6.cloned.1.call-start = ((), (), s32[]{:S(2)}) async-start(), calls=%async_computation.6 | async-start | bytes 18874368 | tf_op jit(solution)/shard_map/all_gather | solution.py:24
  7.3 280.1 %all-gather.8.cloned.1.call-start = ((), (), s32[]{:S(2)}) async-start(), calls=%async_computation.7 | async-start | bytes 4718592 | tf_op jit(solution)/shard_map/all_gather | solution.py:30
  217.9 141.1 %all-gather.4.cloned.1.call-start = ((), (), s32[]{:S(2)}) async-start(), calls=%async_computation.5 | async-start | bytes 4718592 | tf_op jit(solution)/shard_map/all_gather | solution.py:29
  218.6 277.6 %all-reduce.2.cloned.1.call-start = ((), (), s32[]{:S(2)}) async-start(), calls=%async_computation.8 | async-start | bytes 8388608 | tf_op jit(solution)/shard_map/psum | solution.py:32
  287.4 426.3 %reduce-scatter.2.cloned.1.call-start = ((), (), s32[]{:S(2)}) async-start(), calls=%async_computation.9 | async-start | bytes 18874368 | tf_op jit(solution)/shard_map/reduce_scatter | solution.py:36
  500.6 1.9 copy-start
  818.4 6.6 copy-start.1
  818.4 30.9 %all-to-all-start.3 = ((f32[4,2,2,128,256]{3,4,1,2,0:T(8,128)}), f32[4,2,2,128,256]{3,4,1,2,0:T(8,128)}, u32[]{:S(2)}, u32[]{:S(2)}) async-start(f32[4,2,2,128,256]{3,4,1,2,0:T(8,128)} %all_to_all.45), calls=%async_computation.4 | async-start | bytes 4194304 | tf_op jit(solution)/shard_map/all_to_all | solution.py:46
  826.8 24.2 %copy-start.2 = (f32[2,2,128,1024]{2,3,1,0:T(8,128)S(1)}, f32[2,2,128,1024]{2,3,1,0:T(8,128)}, u32[]{:S(2)}) copy-start(f32[2,2,128,1024]{2,3,1,0:T(8,128)} %copy.16) | copy-start | bytes 6291460
Sparse Core Ops, SparseCore 0:
  9.7 187.5 all-gather.5
  218.0 69.2 all-gather.7
  289.7 69.2 all-gather.3
  361.4 134.7 all-reduce.1
  518.7 194.8 reduce-scatter.1
where the time goes:
time: 865 us; the launch traced here: 862 us
  waiting for transfers between devices  683 us (79%)
  blocking collectives  86.6 us (10%)
  matrix products  46.6 us (5%)
  local copies, waits for them, and re-layouts  16.6 us (2%)
  between operations  13.2 us (2%)
  other arithmetic  8.71 us (1%)
    reduce_scatter x1, waiting for transfers between devices, body(): lax.psum_scatter(jnp.einsum('ac,pcb->apb', columns, screened, precision=h...  195 us
    all_gather x1, waiting for transfers between devices, body(): piece = lax.all_gather(integrals, 'vir', axis=2, tiled=True)  187 us
    psum x1, waiting for transfers between devices, body(): whole_sum = lax.psum(gathered[1], ('oi', 'oj'))  137 us
    all_gather x1, waiting for transfers between devices, body(): lax.all_gather(fock_virtual, 'vir', axis=0, tiled=True)  71.4 us
    all_gather x1, waiting for transfers between devices, body(): lax.all_gather(added, 'vir', axis=0, tiled=True)  68.7 us
    all_to_all x1, blocking collectives, body(): lax.all_to_all(residual_here, 'vir', split_axis=2, concat_axis=1, tiled=T...  31.7 us
    all_to_all x1, blocking collectives, body(): lax.all_to_all(sectioned, 'oi', split_axis=0, concat_axis=0, tiled=True)  28.9 us
    all_to_all x1, blocking collectives, body(): lax.all_to_all(swapped[None], 'oj', split_axis=4, concat_axis=0, tiled=True)  26 us
  transfers between devices with their start and end apart: 6, of which 6 were waited for; matrix products, arithmetic and copies ran while one was open for 1% of the time, Pallas kernels for 0%

commit v1 on v0

v1 whole, which is shorter than its diff:
```python
import jax
import jax.numpy as jnp
from jax import lax
from jax.sharding import PartitionSpec as P

BLK = 128
high = lax.Precision.HIGH


def mirror_perm(n):
    return [(a * n + b, b * n + a) for a in range(n) for b in range(n)]


def turn(values, n):
    swapped = jnp.transpose(values, (1, 0, 2, 3))
    sent = lax.all_to_all(swapped, "vir", split_axis=3, concat_axis=2, tiled=True)
    return lax.ppermute(sent, ("oi", "oj"), mirror_perm(n))


def body(amplitudes, integrals, fock_virtual, screening):
    occ = amplitudes.shape[0]
    rows_here = amplitudes.shape[2]
    width = amplitudes.shape[3]
    pairs = occ * occ
    n = lax.axis_size("oi")
    vir_place = lax.axis_index("vir")
    nblocks = rows_here // BLK
    block_rows = lax.dynamic_slice(
        screening[0, 0], (vir_place * nblocks, jnp.int32(0)), (nblocks, width // BLK)
    )
    dense = jnp.repeat(jnp.repeat(block_rows.astype(jnp.float32), BLK, axis=0), BLK, axis=1)
    screened = amplitudes * dense[None, None]
    turned = turn(screened, n)
    turned_integrals = turn(integrals, n)
    partial = jnp.einsum("ijad,ijcd->ac", turned, turned_integrals, precision=high)
    share = lax.psum_scatter(partial, ("vir", "oi", "oj"), scatter_dimension=0, tiled=True)
    place = lax.axis_index("oi") * n + lax.axis_index("oj")
    mine = lax.dynamic_slice_in_dim(fock_virtual, place * share.shape[0], share.shape[0], 0)
    dressed = lax.all_gather(mine - share, ("vir", "oi", "oj"), axis=0, tiled=True)
    both = screened + jnp.transpose(turned, (0, 1, 3, 2))
    half = jnp.einsum("pac,bc->pab", both.reshape(pairs, rows_here, width), dressed, precision=high)
    half = half.reshape(occ, occ, rows_here, width)
    return half + jnp.transpose(turn(half, n), (0, 1, 3, 2))


def solution(mesh):
    placed = (
        P("oi", "oj", "vir", None),
        P("oi", "oj", "vir", None),
        P("vir", None),
        P("oi", "oj", None, None),
    )
    return jax.shard_map(
        body, mesh=mesh, in_specs=placed, out_specs=P("oi", "oj", "vir", None), check_vma=False
    )
```

time: 865 us -> 1250 us (1.45)
  waiting for transfers between devices: 683 us -> 1140 us
  blocking collectives: 86.6 us -> 35.8 us
  matrix products: 46.6 us -> 15.5 us
  starting transfers between devices: 6.94 us -> 23.5 us
    reduce_scatter x1, waiting for transfers between devices: 195 us -> 638 us  [body(): lax.psum_scatter(partial, ('vir', 'oi', 'oj'), scatter_dimension=0, tiled...]
    ppermute x0 -> x3, waiting for transfers between devices: none -> 139 us  [turn(): return lax.ppermute(sent, ('oi', 'oj'), mirror_perm(n))]
    psum x1 -> x0, waiting for transfers between devices: 137 us -> none  [body(): whole_sum = lax.psum(gathered[1], ('oi', 'oj'))]
    all_to_all x3 -> x1, blocking collectives: 86.6 us -> 35.8 us  [turn(): lax.all_to_all(swapped, 'vir', split_axis=3, concat_axis=2, tiled=True)]
    dot_general x3 -> x2, matrix products: 46.6 us -> 15.5 us  [the longest x1 10.3 us: body(): jnp.einsum('pac,bc->pab', both.reshape(pairs, rows_here, width), dressed,...]
    all_to_all x1 -> x2, waiting for transfers between devices: 22.5 us -> 48.9 us  [turn(): lax.all_to_all(swapped, 'vir', split_axis=3, concat_axis=2, tiled=True)]
    all_gather x3 -> x1, waiting for transfers between devices: 327 us -> 310 us  [body(): lax.all_gather(mine - share, ('vir', 'oi', 'oj'), axis=0, tiled=True)]
  transfers between devices with their start and end apart: 6 -> 7, of which waited for: 6 -> 7; matrix products, arithmetic and copies ran while one was open for 1% -> 1% of each run, Pallas kernels for 0% -> 0%
where the time goes in v1:
time: 1250 us
  waiting for transfers between devices  1140 us (91%)
  blocking collectives  35.8 us (3%)
  local copies, waits for them, and re-layouts  25.4 us (2%)
  starting transfers between devices  23.5 us (2%)
  matrix products  15.5 us (1%)
  between operations  13.5 us (1%)
    reduce_scatter x1, waiting for transfers between devices, body(): lax.psum_scatter(partial, ('vir', 'oi', 'oj'), scatter_dimension=0, tiled...  638 us
    all_gather x1, waiting for transfers between devices, body(): lax.all_gather(mine - share, ('vir', 'oi', 'oj'), axis=0, tiled=True)  310 us
    ppermute x3, waiting for transfers between devices, turn(): return lax.ppermute(sent, ('oi', 'oj'), mirror_perm(n))  139 us
    all_to_all x2, waiting for transfers between devices, turn(): lax.all_to_all(swapped, 'vir', split_axis=3, concat_axis=2, tiled=True)  48.9 us
    all_to_all x1, blocking collectives, turn(): lax.all_to_all(swapped, 'vir', split_axis=3, concat_axis=2, tiled=True)  35.8 us
  transfers between devices with their start and end apart: 7, of which 7 were waited for; matrix products, arithmetic and copies ran while one was open for 1% of the time, Pallas kernels for 0%

profile of v1, /device:TPU:24, one launch (start us, length us, event | category | flops | bytes accessed | tf_op | source)
XLA Modules:
  0.0 1252.8 jit_solution(9325854613754523158)
XLA Ops:
  7.3 1.9 copy.15
  10.5 2.9 copy.16
  13.5 7.6 all-to-all-start
  21.1 4.1 copy.18
  25.2 24.3 %all-to-all-done = f32[2,2,128,1024]{2,0,1,3:T(2,128)S(1)} async-done(((f32[2,2,128,1024]{2,0,1,3:T(2,128)}), f32[2,2,128,1024]{2,0,1,3:T(2,128)S(1)}, u32[]{:S(2)}, u32[]{:S(2)}) %all-to-all-start) | async-done | bytes 2097184 | tf_op jit(solution)/shard_map/all_to_all | solution.py:16
  49.5 6.1 all-to-all-start.1
  55.6 2.8 copy.17
  58.4 24.5 %all-to-all-done.1 = f32[2,2,128,1024]{2,1,0,3:T(2,128)} async-done(((f32[2,2,128,1024]{2,1,0,3:T(2,128)}), f32[2,2,128,1024]{2,1,0,3:T(2,128)}, u32[]{:S(2)}, u32[]{:S(2)}) %all-to-all-start.1) | async-done | bytes 2097184 | tf_op jit(solution)/shard_map/all_to_all | solution.py:16
  83.0 1.7 copy.19
  84.7 1.8 copy.20
  86.5 1.9 collective-permute-start.1
  88.4 5.8 collective-permute-start
  94.2 66.5 %collective-permute-done.1 = f32[2,2,1024,128]{3,2,1,0:T(8,128)S(1)} collective-permute-done((f32[2,2,1024,128]{3,2,1,0:T(8,128)}, f32[2,2,1024,128]{3,2,1,0:T(8,128)S(1)}, u32[]{:S(2)}, u32[]{:S(2)}) %collective-permute-start.1) | collective-permute-done | bytes 2097184 | tf_op jit(solution)/shard_map/ppermute | solution.py:17
  160.7 22.5 %collective-permute-done = f32[2,2,1024,128]{3,2,1,0:T(8,128)S(1)} collective-permute-done((f32[2,2,1024,128]{3,2,1,0:T(8,128)}, f32[2,2,1024,128]{3,2,1,0:T(8,128)S(1)}, u32[]{:S(2)}, u32[]{:S(2)}) %collective-permute-start) | collective-permute-done | bytes 2097184 | tf_op jit(solution)/shard_map/ppermute | solution.py:17
  184.5 5.1 convolution_bitcast_fusion
  189.8 637.8 %reduce-scatter.2.cloned.1.call-done = f32[8,1024]{1,0:T(8,128)} async-done(((f32[1024,1024]{1,0:T(8,128)}), f32[8,1024]{1,0:T(8,128)}) %reduce-scatter.2.cloned.1.call-update) | async-done | bytes 32784 | tf_op jit(solution)/shard_map/reduce_scatter | solution.py:36
  828.9 309.7 %all-gather.2.cloned.1.call-done = f32[1024,1024]{1,0:T(8,128)} async-done(((f32[8,1024]{1,0:T(8,128)}), f32[1024,1024]{1,0:T(8,128)}) %all-gather.2.cloned.1.call-update) | async-done | bytes 4194320 | tf_op jit(solution)/shard_map/all_gather | solution.py:39
  1138.6 10.3 fusion
  1149.0 2.3 copy.22
  1151.3 35.8 %all_to_all.54 = f32[2,2,128,1024]{2,0,1,3:T(2,128)S(1)} all-to-all(f32[2,2,128,1024]{2,0,1,3:T(2,128)} %copy.22), channel_id=1, replica_groups=mesh['oi'=4,'oj'=4,'vir'=8] {'vir'}, dimensions={3} | all-to-all | bytes 4194304 | tf_op jit(solution)/shard_map/all_to_all | solution.py:16
  1187.1 2.5 copy.28
  1189.6 2.7 all_to_all.50
  1192.4 2.1 collective-permute-start.2
  1194.4 49.8 %collective-permute-done.2 = f32[2,2,1024,128]{2,3,1,0:T(8,128)S(1)} collective-permute-done((f32[2,2,1024,128]{2,3,1,0:T(8,128)}, f32[2,2,1024,128]{2,3,1,0:T(8,128)S(1)}, u32[]{:S(2)}, u32[]{:S(2)}) %collective-permute-start.2) | collective-permute-done | bytes 2097184 | tf_op jit(solution)/shard_map/ppermute | solution.py:17
  (13 shorter events, 6.6 us)
Async XLA Ops:
  9.2 1.3 copy-start
  13.5 36.1 %all-to-all-start = ((f32[2,2,128,1024]{2,0,1,3:T(2,128)}), f32[2,2,128,1024]{2,0,1,3:T(2,128)S(1)}, u32[]{:S(2)}, u32[]{:S(2)}) async-start(f32[2,2,128,1024]{2,0,1,3:T(2,128)} %copy.16), calls=%async_computation | async-start | bytes 4194304 | tf_op jit(solution)/shard_map/all_to_all | solution.py:16
  49.5 33.4 %all-to-all-start.1 = ((f32[2,2,128,1024]{2,1,0,3:T(2,128)}), f32[2,2,128,1024]{2,1,0,3:T(2,128)}, u32[]{:S(2)}, u32[]{:S(2)}) async-start(f32[2,2,128,1024]{2,1,0,3:T(2,128)} %bitcast.42), calls=%async_computation.1 | async-start | bytes 4194304 | tf_op jit(solution)/shard_map/all_to_all | solution.py:16
  55.6 771.9 %reduce-scatter.2.cloned.1.call-start = ((), (), s32[]{:S(2)}) async-start(), calls=%async_computation.4 | async-start | bytes 4227072 | tf_op jit(solution)/shard_map/reduce_scatter | solution.py:36
  86.5 74.2 %collective-permute-start.1 = (f32[2,2,1024,128]{3,2,1,0:T(8,128)}, f32[2,2,1024,128]{3,2,1,0:T(8,128)S(1)}, u32[]{:S(2)}, u32[]{:S(2)}) collective-permute-start(f32[2,2,1024,128]{3,2,1,0:T(8,128)} %bitcast.47), channel_id=1, source_target_pairs={{0,0},{8,32},{16,64},{24,96},{32,8},{40,40},{48,72},{56,104},{64,1... | collective-permute-start | bytes 6291464 | tf_op jit(solution)/shard_map/ppermute | solution.py:17
  88.4 94.8 %collective-permute-start = (f32[2,2,1024,128]{3,2,1,0:T(8,128)}, f32[2,2,1024,128]{3,2,1,0:T(8,128)S(1)}, u32[]{:S(2)}, u32[]{:S(2)}) collective-permute-start(f32[2,2,1024,128]{3,2,1,0:T(8,128)} %bitcast.46), channel_id=1, source_target_pairs={{0,0},{8,32},{16,64},{24,96},{32,8},{40,40},{48,72},{56,104},{64,1... | collective-permute-start | bytes 6291464 | tf_op jit(solution)/shard_map/ppermute | solution.py:17
  183.2 1.3 copy-start.1
  189.7 948.9 %all-gather.2.cloned.1.call-start = ((), (), s32[]{:S(2)}) async-start(), calls=%async_computation.5 | async-start | bytes 4227072 | tf_op jit(solution)/shard_map/all_gather | solution.py:39
  1192.4 51.9 %collective-permute-start.2 = (f32[2,2,1024,128]{2,3,1,0:T(8,128)}, f32[2,2,1024,128]{2,3,1,0:T(8,128)S(1)}, u32[]{:S(2)}, u32[]{:S(2)}) collective-permute-start(f32[2,2,1024,128]{2,3,1,0:T(8,128)} %all_to_all.50), channel_id=1, source_target_pairs={{0,0},{8,32},{16,64},{24,96},{32,8},{40,40},{48,72},{56,104},{64,1... | collective-permute-start | bytes 6291464 | tf_op jit(solution)/shard_map/ppermute | solution.py:17
Sparse Core Ops, SparseCore 0:
  189.8 637.6 reduce-scatter.1
  829.2 309.3 all-gather.1

commit v2 on v1

v2 whole, which is shorter than its diff:
```python
import functools

import jax
import jax.numpy as jnp
from jax import lax
from jax.experimental import pallas as pl
from jax.experimental.pallas import tpu as pltpu
from jax.sharding import PartitionSpec as P

BLK = 128
MESH = pl.DeviceIdType.MESH
high = lax.Precision.HIGH
COLORS = ((0, 384), (384, 384), (768, 256))


def places():
    return lax.axis_index("oi"), lax.axis_index("oj"), lax.axis_index("vir")


def ring_places(v):
    half, x = v // 4, v % 4
    order = ((1, 2), (0, 2), (1, 1), (1, 3), (0, 1), (0, 3), (1, 0), (0, 0))
    return [((half + dh) % 2) * 4 + (x + dx) % 4 for dh, dx in order]


def turn_kernel(count, *refs):
    sources, targets = refs[:count], refs[count : 2 * count]
    send_sem, recv_sem, own_sem = refs[2 * count :]
    oi, oj, v = places()
    others = ring_places(v)
    apart = jnp.where(oi == oj, 0, 1)
    barrier = pltpu.get_barrier_semaphore()
    for w in others[:-1]:
        pl.semaphore_signal(barrier, inc=1, device_id=(oj, oi, w), device_id_type=MESH)

    @pl.when(oi != oj)
    def _():
        pl.semaphore_signal(barrier, inc=1, device_id=(oj, oi, v), device_id_type=MESH)

    pl.semaphore_wait(barrier, 7 + apart)

    def remote(k, w, frm):
        return pltpu.make_async_remote_copy(
            src_ref=sources[k].at[:, :, pl.ds(pl.multiple_of(w * BLK, BLK), BLK)],
            dst_ref=targets[k].at[:, pl.ds(pl.multiple_of(frm * BLK, BLK), BLK), :],
            send_sem=send_sem.at[k, w],
            recv_sem=recv_sem.at[k, frm],
            device_id=(oj, oi, w),
            device_id_type=MESH,
        )

    def own(k):
        return pltpu.make_async_copy(
            sources[k].at[:, :, pl.ds(pl.multiple_of(v * BLK, BLK), BLK)],
            targets[k].at[:, pl.ds(pl.multiple_of(v * BLK, BLK), BLK), :],
            own_sem.at[k],
        )

    for k in range(count):
        for w in others[:-1]:
            remote(k, w, v).start()

        @pl.when(oi != oj)
        def _():
            remote(k, v, v).start()

        @pl.when(oi == oj)
        def _():
            own(k).start()

    for k in range(count):
        for w in others[:-1]:
            remote(k, w, w).wait_recv()
            remote(k, w, v).wait_send()

        @pl.when(oi != oj)
        def _():
            remote(k, v, v).wait()

        @pl.when(oi == oj)
        def _():
            own(k).wait()


def turn(cid, *arrays):
    count = len(arrays)
    pairs, rows, width = arrays[0].shape
    vmem = pl.BlockSpec(memory_space=pltpu.VMEM)
    return pl.pallas_call(
        functools.partial(turn_kernel, count),
        out_shape=[jax.ShapeDtypeStruct((pairs, width, rows), jnp.float32)] * count,
        in_specs=[vmem] * count,
        out_specs=[vmem] * count,
        scratch_shapes=[
            pltpu.SemaphoreType.DMA((count, 8)),
            pltpu.SemaphoreType.DMA((count, 8)),
            pltpu.SemaphoreType.DMA((count,)),
        ],
        compiler_params=pltpu.CompilerParams(collective_id=cid, has_side_effects=True),
        name=f"turn{count}",
    )(*arrays)


def gray_bits(p):
    return ((p + 1) // 2) % 2, p // 2


def dressing_kernel(p_ref, fock_ref, d_ref, acc, got, core_got, rs_send, rs_recv, ag_send, ag_recv):
    oi, oj, v = places()
    core, low = oi % 2, oi // 2
    half, x = v // 4, v % 4
    z = half * 2 + low
    bits = [gray_bits(x), gray_bits(oj), gray_bits(z)]
    first = [
        (oi, oj, half * 4 + x + 1 - 2 * (x % 2)),
        (oi, oj + 1 - 2 * (oj % 2), v),
        ((oi + 2) % 4, oj, v),
    ]
    second = [
        (oi, oj, half * 4 + 3 - x),
        (oi, 3 - oj, v),
        ((oi + 2) % 4, oj, (v + 4) % 8),
    ]
    twin = (oi + 1 - 2 * core, oj, v)

    barrier = pltpu.get_barrier_semaphore()
    for peer in [twin] + first + second:
        pl.semaphore_signal(barrier, inc=1, device_id=peer, device_id_type=MESH)
    pl.semaphore_wait(barrier, 7)

    def step(g, k):
        j = (g + k) % 6
        axis = j % 3
        letter = (j // 3 + core) % 2
        peer = tuple(a + letter * (b - a) for a, b in zip(first[axis], second[axis]))
        bit = bits[axis][0] + letter * (bits[axis][1] - bits[axis][0])
        return peer, bit

    def rows(start, size):
        return pl.ds(pl.multiple_of(start, 8), size)

    def core_copy(g):
        c0, cn = COLORS[g]
        return pltpu.make_async_remote_copy(
            src_ref=p_ref.at[rows((1 - core) * 512, 512), pl.ds(c0, cn)],
            dst_ref=core_got.at[:, pl.ds(c0, cn)],
            send_sem=rs_send.at[0, g],
            recv_sem=rs_recv.at[0, g],
            device_id=twin,
            device_id_type=MESH,
        )

    def rs_copy(g, k, start):
        c0, cn = COLORS[g]
        size = 256 >> k
        peer, bit = step(g, k)
        return pltpu.make_async_remote_copy(
            src_ref=acc.at[rows(start + (1 - bit) * size, size), pl.ds(c0, cn)],
            dst_ref=got.at[pl.ds(size, size), pl.ds(c0, cn)],
            send_sem=rs_send.at[k + 1, g],
            recv_sem=rs_recv.at[k + 1, g],
            device_id=peer,
            device_id_type=MESH,
        )

    def ag_copy(g, k, start, place):
        c0, cn = COLORS[g]
        size = 256 >> k
        peer, _ = step(g, k)
        here = d_ref.at[rows(core * 512 + start + place * size, size), pl.ds(c0, cn)]
        return pltpu.make_async_remote_copy(
            src_ref=here,
            dst_ref=here,
            send_sem=ag_send.at[k + 1, g],
            recv_sem=ag_recv.at[k + 1, g],
            device_id=peer,
            device_id_type=MESH,
        )

    def core_back(g, which):
        c0, cn = COLORS[g]
        here = d_ref.at[rows(which * 512, 512), pl.ds(c0, cn)]
        return pltpu.make_async_remote_copy(
            src_ref=here,
            dst_ref=here,
            send_sem=ag_send.at[0, g],
            recv_sem=ag_recv.at[0, g],
            device_id=twin,
            device_id_type=MESH,
        )

    colours = range(3)
    for g in colours:
        core_copy(g).start()
    starts = [[jnp.int32(0)] for _ in colours]
    for g in colours:
        c0, cn = COLORS[g]
        core_copy(g).wait_recv()
        acc[:, pl.ds(c0, cn)] = p_ref[rows(core * 512, 512), pl.ds(c0, cn)] + core_got[:, pl.ds(c0, cn)]

        @pl.when((oj == 0) & (oi == half))
        def _():
            acc[rows(x * BLK, BLK), pl.ds(c0, cn)] -= fock_ref[:, pl.ds(c0, cn)]

        rs_copy(g, 0, starts[g][0]).start()
    for k in range(6):
        size = 256 >> k
        for g in colours:
            c0, cn = COLORS[g]
            _, bit = step(g, k)
            rs_copy(g, k, starts[g][k]).wait_recv()
            mine = starts[g][k] + bit * size
            starts[g].append(mine)
            total = acc[rows(mine, size), pl.ds(c0, cn)] + got[pl.ds(size, size), pl.ds(c0, cn)]
            if k < 5:
                acc[rows(mine, size), pl.ds(c0, cn)] = total
                rs_copy(g, k + 1, mine).start()
            else:
                d_ref[rows(core * 512 + mine, size), pl.ds(c0, cn)] = -total
                _, bit = step(g, 5)
                ag_copy(g, 5, starts[g][5], bit).start()
    for k in range(5, -1, -1):
        for g in colours:
            _, bit = step(g, k)
            ag_copy(g, k, starts[g][k], 1 - bit).wait_recv()
            if k > 0:
                _, bit = step(g, k - 1)
                ag_copy(g, k - 1, starts[g][k - 1], bit).start()
            else:
                core_back(g, core).start()
    for g in colours:
        core_back(g, 1 - core).wait_recv()
    for g in colours:
        core_copy(g).wait_send()
        core_back(g, core).wait_send()
        for k in range(6):
            _, bit = step(g, k)
            rs_copy(g, k, starts[g][k]).wait_send()
            ag_copy(g, k, starts[g][k], bit).wait_send()


def dressing(partial, fock):
    vmem = pl.BlockSpec(memory_space=pltpu.VMEM)
    size = partial.shape[0]
    return pl.pallas_call(
        dressing_kernel,
        out_shape=jax.ShapeDtypeStruct((size, size), jnp.float32),
        in_specs=[vmem] * 2,
        out_specs=vmem,
        scratch_shapes=[
            pltpu.VMEM((512, 1024), jnp.float32),
            pltpu.VMEM((512, 1024), jnp.float32),
            pltpu.VMEM((512, 1024), jnp.float32),
            pltpu.SemaphoreType.DMA((7, 3)),
            pltpu.SemaphoreType.DMA((7, 3)),
            pltpu.SemaphoreType.DMA((7, 3)),
            pltpu.SemaphoreType.DMA((7, 3)),
        ],
        compiler_params=pltpu.CompilerParams(collective_id=1, has_side_effects=True),
        name="dressing",
    )(partial, fock)


def body(amplitudes, integrals, fock_virtual, screening):
    occ = amplitudes.shape[0]
    rows_here = amplitudes.shape[2]
    width = amplitudes.shape[3]
    pairs = occ * occ
    vir_place = lax.axis_index("vir")
    block_rows = lax.dynamic_slice(screening[0, 0], (vir_place, jnp.int32(0)), (1, width // BLK))
    dense = jnp.repeat(block_rows.astype(jnp.float32), BLK, axis=1)
    screened = amplitudes.reshape(pairs, rows_here, width) * dense[None]
    turned, turned_integrals = turn(2, screened, integrals.reshape(pairs, rows_here, width))
    partial = jnp.einsum("pad,pcd->ac", turned, turned_integrals, precision=high)
    dressed = dressing(partial, fock_virtual)

    def mirrored(values):
        values = values.reshape(occ, occ, width, rows_here)
        return jnp.transpose(values, (1, 0, 3, 2)).reshape(pairs, rows_here, width)

    both = screened + mirrored(turned)
    term = jnp.einsum("pac,bc->pab", both, dressed, precision=high)
    (back,) = turn(3, term)
    out = term + mirrored(back)
    return out.reshape(occ, occ, rows_here, width)


def solution(mesh):
    placed = (
        P("oi", "oj", "vir", None),
        P("oi", "oj", "vir", None),
        P("vir", None),
        P("oi", "oj", None, None),
    )
    return jax.shard_map(
        body, mesh=mesh, in_specs=placed, out_specs=P("oi", "oj", "vir", None), check_vma=False
    )
```

time: 1250 us -> 252 us (0.20)
  waiting for transfers between devices: 1140 us -> 0 us
  Pallas kernels: 0 us -> 221 us
  blocking collectives: 35.8 us -> 0 us
  starting transfers between devices: 23.5 us -> 0 us
  local copies, waits for them, and re-layouts: 25.4 us -> 6.18 us
  between operations: 13.5 us -> 0.06 us
    reduce_scatter x1 -> x0, waiting for transfers between devices: 638 us -> none  [body(): lax.psum_scatter(partial, ('vir', 'oi', 'oj'), scatter_dimension=0, tiled...]
    all_gather x1 -> x0, waiting for transfers between devices: 310 us -> none  [body(): lax.all_gather(mine - share, ('vir', 'oi', 'oj'), axis=0, tiled=True)]
    pallas_call x0 -> x3, Pallas kernels: none -> 221 us  [the longest x2 159 us: turn(): pl.pallas_call(functools.partial(turn_kernel, count), out_shape=[jax.Shap...]
    ppermute x3 -> x0, waiting for transfers between devices: 139 us -> none  [turn(): return lax.ppermute(sent, ('oi', 'oj'), mirror_perm(n))]
    all_to_all x2 -> x0, waiting for transfers between devices: 48.9 us -> none  [turn(): lax.all_to_all(swapped, 'vir', split_axis=3, concat_axis=2, tiled=True)]
    all_to_all x1 -> x0, blocking collectives: 35.8 us -> none  [turn(): lax.all_to_all(swapped, 'vir', split_axis=3, concat_axis=2, tiled=True)]
    all_to_all x2 -> x0, starting transfers between devices: 13.7 us -> none  [turn(): lax.all_to_all(swapped, 'vir', split_axis=3, concat_axis=2, tiled=True)]
  transfers between devices with their start and end apart: 7 -> 0, of which waited for: 7 -> 0; matrix products, arithmetic and copies ran while one was open for 1% -> 0% of each run, Pallas kernels for 0% -> 0%
where the time goes in v2:
time: 252 us; the launch traced here: 250 us
  Pallas kernels  221 us (88%)
  matrix products  12.1 us (5%)
  other arithmetic  10.8 us (4%)
  local copies, waits for them, and re-layouts  6.18 us (2%)
    pallas_call x2, Pallas kernels, turn(): pl.pallas_call(functools.partial(turn_kernel, count), out_shape=[jax.Shap...  159 us
    pallas_call x1, Pallas kernels, dressing(): pl.pallas_call(dressing_kernel, out_shape=jax.ShapeDtypeStruct((size, siz...  61.8 us
    dot_general x1, matrix products, body(): term = jnp.einsum('pac,bc->pab', both, dressed, precision=high)  6.99 us
    dot_general x1, matrix products, body(): jnp.einsum('pad,pcd->ac', turned, turned_integrals, precision=high)  5.12 us

profile of v2, /device:TPU:24, one launch (start us, length us, event | category | flops | bytes accessed | tf_op | source)
XLA Modules:
  0.0 249.8 jit_solution(15329860662688484785)
XLA Ops:
  0.0 0.7 convert_bitcast_fusion
  0.7 0.1 broadcast_bitcast_fusion
  0.8 3.3 %bitcast_multiply_fusion.refs_0_ = f32[4,128,1024]{2,1,0:T(8,128)} fusion(f32[2,2,128,1024]{3,2,1,0:T(8,128)} %param.4, f32[1024]{0:T(1024)S(1)} %broadcast_bitcast_fusion), kind=kLoop, calls=%fused_computation.5 | loop fusion | flops 524288 | bytes 4198400 | tf_op jit(solution)/shard_map/mul | solution.py:272
  4.0 103.9 %turn2.1 = (f32[4,1024,128]{2,1,0:T(8,128)}, f32[4,1024,128]{2,1,0:T(8,128)}) custom-call(f32[4,128,1024]{2,1,0:T(8,128)} %bitcast_multiply_fusion.refs_0_, f32[4,128,1024]{2,1,0:T(8,128)} %bitcast.30), custom_call_target="tpu_custom_call" | custom-call | tf_op jit(solution)/shard_map/turn2/pallas_call | solution.py:89
  107.9 0.0 copy-start.1
  107.9 3.0 %copy.5 = f32[2,2,1024,128]{2,3,0,1:T(8,128)} copy(f32[2,2,1024,128]{3,2,1,0:T(8,128)} %bitcast.29) | data formatting | bytes 4194304 | tf_op jit(solution)/shard_map/reshape | solution.py:278
  111.0 0.0 copy-done.1
  111.0 0.0 copy-start.2
  111.0 0.0 copy-start.4
  111.0 3.6 %bitcast_add_fusion = f32[4,128,1024]{2,1,0:T(8,128)} fusion(f32[2,2,1024,128]{2,3,0,1:T(8,128)} %copy.5, f32[1024]{0:T(1024)S(1)} %broadcast_bitcast_fusion, f32[2,2,128,1024]{3,2,1,0:T(8,128)S(1)} %copy-done.1), kind=kLoop, calls=%fused_computation.3 | loop fusion | flops 1048576 | bytes 6295552 | tf_op jit(solution)/shard_map/add | solution.py:281
  114.5 0.0 copy-done.2
  114.5 0.0 copy-done.4
  114.5 5.1 %convolution_bitcast_fusion.p_ref = f32[1024,1024]{1,0:T(8,128)} fusion(f32[4,1024,128]{2,1,0:T(8,128)S(1)} %copy-done.2, f32[4,1024,128]{2,1,0:T(8,128)S(1)} %copy-done.4), kind=kOutput, calls=%fused_computation.2 | convolution fusion | flops 3221225472 | bytes 8388608 | tf_op jit(solution)/shard_map/pad,pcd->ac/dot_general | solution.py:274
  119.7 0.0 copy-start.3
  119.7 61.8 %dressing.1 = f32[1024,1024]{1,0:T(8,128)} custom-call(f32[1024,1024]{1,0:T(8,128)} %convolution_bitcast_fusion.p_ref, f32[128,1024]{1,0:T(8,128)} %fock_ref.1), custom_call_target="tpu_custom_call" | custom-call | tf_op jit(solution)/shard_map/dressing/pallas_call | solution.py:245
  181.4 0.0 copy-done.3
  181.5 7.0 %fusion.refs_0_ = f32[4,128,1024]{2,1,0:T(8,128)} fusion(f32[4,128,1024]{2,1,0:T(8,128)S(1)} %copy-done.3, f32[1024,1024]{1,0:T(8,128)} %dressing.1), kind=kOutput, calls=%fused_computation | convolution fusion | flops 3221225472 | bytes 8388608 | tf_op jit(solution)/shard_map/pac,bc->pab/dot_general | solution.py:282
  188.4 55.0 %turn1.1 = f32[4,1024,128]{2,1,0:T(8,128)} custom-call(f32[4,128,1024]{2,1,0:T(8,128)} %fusion.refs_0_), custom_call_target="tpu_custom_call" | custom-call | tf_op jit(solution)/shard_map/turn1/pallas_call | solution.py:89
  243.5 0.0 copy-start
  243.5 3.0 %copy.6 = f32[2,2,128,1024]{3,2,1,0:T(8,128)} copy(f32[2,2,128,1024]{2,3,0,1:T(8,128)} %bitcast.28) | data formatting | bytes 4194304 | tf_op jit(solution)/shard_map/transpose | solution.py:279
  246.5 0.0 copy-done
  246.5 3.3 %bitcast_add_fusion.1 = f32[4,128,1024]{2,1,0:T(8,128)} fusion(f32[4,128,1024]{2,1,0:T(8,128)S(1)} %copy-done, f32[2,2,128,1024]{3,2,1,0:T(8,128)} %copy.6), kind=kLoop, calls=%fused_computation.4 | loop fusion | flops 524288 | bytes 6291456 | tf_op jit(solution)/shard_map/add | solution.py:284
Async XLA Ops:
  107.9 3.1 %copy-start.1 = (f32[2,2,128,1024]{3,2,1,0:T(8,128)S(1)}, f32[2,2,128,1024]{3,2,1,0:T(8,128)}, u32[]{:S(2)}) copy-start(f32[2,2,128,1024]{3,2,1,0:T(8,128)} %param.4) | copy-start | bytes 6291460
  111.0 3.6 %copy-start.2 = (f32[4,1024,128]{2,1,0:T(8,128)S(1)}, f32[4,1024,128]{2,1,0:T(8,128)}, u32[]{:S(2)}) copy-start(f32[4,1024,128]{2,1,0:T(8,128)} %get-tuple-element.7) | copy-start | bytes 6291460
  111.0 3.6 %copy-start.4 = (f32[4,1024,128]{2,1,0:T(8,128)S(1)}, f32[4,1024,128]{2,1,0:T(8,128)}, u32[]{:S(2)}) copy-start(f32[4,1024,128]{2,1,0:T(8,128)} %get-tuple-element.8) | copy-start | bytes 6291460
  119.7 61.8 %copy-start.3 = (f32[4,128,1024]{2,1,0:T(8,128)S(1)}, f32[4,128,1024]{2,1,0:T(8,128)}, u32[]{:S(2)}) copy-start(f32[4,128,1024]{2,1,0:T(8,128)} %bitcast_add_fusion) | copy-start | bytes 6291460
  243.5 3.1 %copy-start = (f32[4,128,1024]{2,1,0:T(8,128)S(1)}, f32[4,128,1024]{2,1,0:T(8,128)}, u32[]{:S(2)}) copy-start(f32[4,128,1024]{2,1,0:T(8,128)} %fusion.refs_0_) | copy-start | bytes 6291460

commit v3 on v2

--- a/solution.py
+++ b/solution.py
@@ -17,69 +17,189 @@
     return lax.axis_index("oi"), lax.axis_index("oj"), lax.axis_index("vir")
 
 
-def ring_places(v):
-    half, x = v // 4, v % 4
-    order = ((1, 2), (0, 2), (1, 1), (1, 3), (0, 1), (0, 3), (1, 0), (0, 0))
-    return [((half + dh) % 2) * 4 + (x + dx) % 4 for dh, dx in order]
+ORDER = ((1, 2), (0, 2), (1, 1), (1, 3), (0, 1), (0, 3), (1, 0), (0, 0))
+PARTS = 2
+
+
+def ring_place(v, dh, dx):
+    return ((v // 4 + dh % 2) % 2) * 4 + (v % 4 + dx % 4) % 4
+
+
+class Turn:
+    def __init__(self, sources, targets, holds, sems):
+        self.sources, self.targets, self.holds = sources, targets, holds
+        self.send, self.recv, self.hold_recv, self.forward_send, self.own_sem = sems
+        self.oi, self.oj, self.v = places()
+        self.same = self.oi == self.oj
+        self.apart = (self.oi + 2) % 4 == self.oj
+        self.cross = self.oi + self.oj == 3
+        self.plain = jnp.logical_not(self.same | self.apart)
+
+    def greet(self):
+        oi, oj, v = self.oi, self.oj, self.v
+        barrier = pltpu.get_barrier_semaphore()
+
+        def signal(a, b, w):
+            pl.semaphore_signal(barrier, inc=1, device_id=(a, b, w), device_id_type=MESH)
+
+        def everyone(a, b, itself):
+            for dh, dx in ORDER if itself else ORDER[:-1]:
+                signal(a, b, ring_place(v, dh, dx))
+
+        @pl.when(self.same)
+        def _():
+            everyone(oi, oi, False)
+            everyone((oi + 2) % 4, oi, True)
+            signal(oi, 3 - oi, v)
+
+        @pl.when(self.apart)
+        def _():
+            everyone(oj, oj, True)
+            signal(oi, 3 - oi, v)
+
+        @pl.when(self.plain)
+        def _():
+            everyone(oj, oi, True)
+
+            @pl.when(self.cross)
+            def _():
+                signal(oi, oi, v)
+                signal(oi, (oi + 2) % 4, v)
+
+        pl.semaphore_wait(
+            barrier,
+            jnp.where(self.same, 16, jnp.where(self.apart, 9, jnp.where(self.cross, 10, 8))),
+        )
+
+    def tile(self, k, w, part):
+        pairs = self.sources[k].shape[0] // PARTS
+        return self.sources[k].at[pl.ds(part * pairs, pairs), :, pl.ds(pl.multiple_of(w * BLK, BLK), BLK)]
+
+    def slot(self, array, frm, part):
+        pairs = array.shape[0] // PARTS
+        return array.at[pl.ds(part * pairs, pairs), pl.ds(pl.multiple_of(frm * BLK, BLK), BLK), :]
+
+    def straight(self, k, w, frm, part):
+        return pltpu.make_async_remote_copy(
+            src_ref=self.tile(k, w, part),
+            dst_ref=self.slot(self.targets[k], frm, part),
+            send_sem=self.send.at[k, w, part],
+            recv_sem=self.recv.at[k, frm, part],
+            device_id=(self.oj, self.oi, w),
+            device_id_type=MESH,
+        )
+
+    def detour(self, k, w, part):
+        return pltpu.make_async_remote_copy(
+            src_ref=self.tile(k, w, part),
+            dst_ref=self.slot(self.holds[k], self.v, part),
+            send_sem=self.send.at[k, w, part],
+            recv_sem=self.hold_recv.at[k, self.v, part],
+            device_id=(self.oj, self.oj, w),
+            device_id_type=MESH,
+        )
+
+    def forward(self, k, frm, part, last):
+        return pltpu.make_async_remote_copy(
+            src_ref=self.slot(self.holds[k], frm, part),
+            dst_ref=self.slot((self.targets if last else self.holds)[k], frm, part),
+            send_sem=self.forward_send.at[k, frm, part],
+            recv_sem=(self.recv if last else self.hold_recv).at[k, frm, part],
+            device_id=(self.oi, (self.oi + 2) % 4 if last else 3 - self.oi, self.v),
+            device_id_type=MESH,
+        )
+
+    def own(self, k):
+        return pltpu.make_async_copy(
+            self.sources[k].at[:, :, pl.ds(pl.multiple_of(self.v * BLK, BLK), BLK)],
+            self.targets[k].at[:, pl.ds(pl.multiple_of(self.v * BLK, BLK), BLK), :],
+            self.own_sem.at[k],
+        )
+
+    def start(self, k):
+        @pl.when(self.apart)
+        def _():
+            for dh, dx in ORDER:
+                for part in range(PARTS):
+                    self.detour(k, ring_place(self.v, dh, dx), part).start()
+
+        @pl.when(self.plain)
+        def _():
+            for dh, dx in ORDER:
+                for part in range(PARTS):
+                    self.straight(k, ring_place(self.v, dh, dx), self.v, part).start()
+
+        @pl.when(self.same)
+        def _():
+            for dh, dx in ORDER[:-1]:
+                for part in range(PARTS):
+                    self.straight(k, ring_place(self.v, dh, dx), self.v, part).start()
+            self.own(k).start()
+
+    def relay(self, k, j):
+        dh, dx = ORDER[j]
+        frm = ring_place(self.v, -dh, -dx)
+        for part in range(PARTS):
+
+            @pl.when(self.same)
+            def _():
+                self.forward(k, frm, part, False).wait_recv()
+                self.forward(k, frm, part, False).start()
+
+            @pl.when(self.cross)
+            def _():
+                self.forward(k, frm, part, False).wait_recv()
+                self.forward(k, frm, part, True).start()
+
+    def arrive(self, k, j):
+        dh, dx = ORDER[j]
+        frm = ring_place(self.v, -dh, -dx)
+
+        def wait():
+            for part in range(PARTS):
+                self.straight(k, frm, frm, part).wait_recv()
+
+        if j < len(ORDER) - 1:
+            wait()
+        else:
+            pl.when(self.same)(lambda: self.own(k).wait())
+            pl.when(jnp.logical_not(self.same))(wait)
+
+    def drain(self, k):
+        for j, (dh, dx) in enumerate(ORDER):
+            w = ring_place(self.v, dh, dx)
+            for part in range(PARTS):
+                if j < len(ORDER) - 1:
+                    self.straight(k, w, w, part).wait_send()
+                else:
+
+                    @pl.when(jnp.logical_not(self.same))
+                    def _():
+                        self.straight(k, w, w, part).wait_send()
+
+                @pl.when(self.same | self.cross)
+                def _():
+                    self.forward(k, w, part, True).wait_send()
+
+
+def turn_sems(count):
+    shape = (count, 8, PARTS)
+    return [pltpu.SemaphoreType.DMA(shape)] * 4 + [pltpu.SemaphoreType.DMA((count,))]
 
 
 def turn_kernel(count, *refs):
-    sources, targets = refs[:count], refs[count : 2 * count]
-    send_sem, recv_sem, own_sem = refs[2 * count :]
-    oi, oj, v = places()
-    others = ring_places(v)
-    apart = jnp.where(oi == oj, 0, 1)
-    barrier = pltpu.get_barrier_semaphore()
-    for w in others[:-1]:
-        pl.semaphore_signal(barrier, inc=1, device_id=(oj, oi, w), device_id_type=MESH)
-
-    @pl.when(oi != oj)
-    def _():
-        pl.semaphore_signal(barrier, inc=1, device_id=(oj, oi, v), device_id_type=MESH)
-
-    pl.semaphore_wait(barrier, 7 + apart)
-
-    def remote(k, w, frm):
-        return pltpu.make_async_remote_copy(
-            src_ref=sources[k].at[:, :, pl.ds(pl.multiple_of(w * BLK, BLK), BLK)],
-            dst_ref=targets[k].at[:, pl.ds(pl.multiple_of(frm * BLK, BLK), BLK), :],
-            send_sem=send_sem.at[k, w],
-            recv_sem=recv_sem.at[k, frm],
-            device_id=(oj, oi, w),
-            device_id_type=MESH,
-        )
-
-    def own(k):
-        return pltpu.make_async_copy(
-            sources[k].at[:, :, pl.ds(pl.multiple_of(v * BLK, BLK), BLK)],
-            targets[k].at[:, pl.ds(pl.multiple_of(v * BLK, BLK), BLK), :],
-            own_sem.at[k],
-        )
-
+    sources, targets, holds = refs[:count], refs[count : 2 * count], refs[2 * count : 3 * count]
+    moves = Turn(sources, targets, holds, refs[3 * count :])
+    moves.greet()
     for k in range(count):
-        for w in others[:-1]:
-            remote(k, w, v).start()
-
-        @pl.when(oi != oj)
-        def _():
-            remote(k, v, v).start()
-
-        @pl.when(oi == oj)
-        def _():
-            own(k).start()
-
+        moves.start(k)
     for k in range(count):
-        for w in others[:-1]:
-            remote(k, w, w).wait_recv()
-            remote(k, w, v).wait_send()
-
-        @pl.when(oi != oj)
-        def _():
-            remote(k, v, v).wait()
-
-        @pl.when(oi == oj)
-        def _():
-            own(k).wait()
+        for j in range(8):
+            moves.relay(k, j)
+    for k in range(count):
+        for j in range(8):
+            moves.arrive(k, j)
+        moves.drain(k)
 
 
 def turn(cid, *arrays):
@@ -91,11 +211,7 @@
         out_shape=[jax.ShapeDtypeStruct((pairs, width, rows), jnp.float32)] * count,
         in_specs=[vmem] * count,
         out_specs=[vmem] * count,
-        scratch_shapes=[
-            pltpu.SemaphoreType.DMA((count, 8)),
-            pltpu.SemaphoreType.DMA((count, 8)),
-            pltpu.SemaphoreType.DMA((count,)),
-        ],
+        scratch_shapes=[pltpu.VMEM((pairs, width, rows), jnp.float32)] * count + turn_sems(count),
         compiler_params=pltpu.CompilerParams(collective_id=cid, has_side_effects=True),
         name=f"turn{count}",
     )(*arrays)

time: 252 us -> 242 us (0.960)
  Pallas kernels: 221 us -> 211 us
    pallas_call x2, Pallas kernels: 159 us -> 149 us  [turn(): pl.pallas_call(functools.partial(turn_kernel, count), out_shape=[jax.Shap...]
where the time goes in v3:
time: 242 us; the launch traced here: 240 us
  Pallas kernels  211 us (87%)
  matrix products  12.1 us (5%)
  other arithmetic  10.8 us (4%)
  local copies, waits for them, and re-layouts  6.18 us (3%)
    pallas_call x2, Pallas kernels, turn(): pl.pallas_call(functools.partial(turn_kernel, count), out_shape=[jax.Shap...  149 us
    pallas_call x1, Pallas kernels, dressing(): pl.pallas_call(dressing_kernel, out_shape=jax.ShapeDtypeStruct((size, siz...  61.8 us
    dot_general x1, matrix products, body(): term = jnp.einsum('pac,bc->pab', both, dressed, precision=high)  6.99 us
    dot_general x1, matrix products, body(): jnp.einsum('pad,pcd->ac', turned, turned_integrals, precision=high)  5.1 us

profile of v3, /device:TPU:24, one launch (start us, length us, event | category | flops | bytes accessed | tf_op | source)
XLA Modules:
  0.0 239.8 jit_solution(2479728156277038508)
XLA Ops:
  0.0 0.7 convert_bitcast_fusion
  0.7 0.1 broadcast_bitcast_fusion
  0.8 3.3 %bitcast_multiply_fusion.refs_0_ = f32[4,128,1024]{2,1,0:T(8,128)} fusion(f32[2,2,128,1024]{3,2,1,0:T(8,128)} %param.4, f32[1024]{0:T(1024)S(1)} %broadcast_bitcast_fusion), kind=kLoop, calls=%fused_computation.5 | loop fusion | flops 524288 | bytes 4198400 | tf_op jit(solution)/shard_map/mul | solution.py:388
  4.0 96.7 %turn2.1 = (f32[4,1024,128]{2,1,0:T(8,128)}, f32[4,1024,128]{2,1,0:T(8,128)}) custom-call(f32[4,128,1024]{2,1,0:T(8,128)} %bitcast_multiply_fusion.refs_0_, f32[4,128,1024]{2,1,0:T(8,128)} %bitcast.30), custom_call_target="tpu_custom_call" | custom-call | tf_op jit(solution)/shard_map/turn2/pallas_call | solution.py:209
  100.7 0.0 copy-start.1
  100.7 3.0 %copy.5 = f32[2,2,1024,128]{2,3,0,1:T(8,128)} copy(f32[2,2,1024,128]{3,2,1,0:T(8,128)} %bitcast.29) | data formatting | bytes 4194304 | tf_op jit(solution)/shard_map/reshape | solution.py:394
  103.8 0.0 copy-done.1
  103.8 0.0 copy-start.2
  103.8 0.0 copy-start.4
  103.8 3.6 %bitcast_add_fusion = f32[4,128,1024]{2,1,0:T(8,128)} fusion(f32[2,2,1024,128]{2,3,0,1:T(8,128)} %copy.5, f32[1024]{0:T(1024)S(1)} %broadcast_bitcast_fusion, f32[2,2,128,1024]{3,2,1,0:T(8,128)S(1)} %copy-done.1), kind=kLoop, calls=%fused_computation.3 | loop fusion | flops 1048576 | bytes 6295552 | tf_op jit(solution)/shard_map/add | solution.py:397
  107.4 0.0 copy-done.2
  107.4 0.0 copy-done.4
  107.4 5.1 %convolution_bitcast_fusion.p_ref = f32[1024,1024]{1,0:T(8,128)} fusion(f32[4,1024,128]{2,1,0:T(8,128)S(1)} %copy-done.2, f32[4,1024,128]{2,1,0:T(8,128)S(1)} %copy-done.4), kind=kOutput, calls=%fused_computation.2 | convolution fusion | flops 3221225472 | bytes 8388608 | tf_op jit(solution)/shard_map/pad,pcd->ac/dot_general | solution.py:390
  112.5 0.0 copy-start.3
  112.5 61.8 %dressing.1 = f32[1024,1024]{1,0:T(8,128)} custom-call(f32[1024,1024]{1,0:T(8,128)} %convolution_bitcast_fusion.p_ref, f32[128,1024]{1,0:T(8,128)} %fock_ref.1), custom_call_target="tpu_custom_call" | custom-call | tf_op jit(solution)/shard_map/dressing/pallas_call | solution.py:361
  174.3 0.0 copy-done.3
  174.3 7.0 %fusion.refs_0_ = f32[4,128,1024]{2,1,0:T(8,128)} fusion(f32[4,128,1024]{2,1,0:T(8,128)S(1)} %copy-done.3, f32[1024,1024]{1,0:T(8,128)} %dressing.1), kind=kOutput, calls=%fused_computation | convolution fusion | flops 3221225472 | bytes 8388608 | tf_op jit(solution)/shard_map/pac,bc->pab/dot_general | solution.py:398
  181.3 52.1 %turn1.1 = f32[4,1024,128]{2,1,0:T(8,128)} custom-call(f32[4,128,1024]{2,1,0:T(8,128)} %fusion.refs_0_), custom_call_target="tpu_custom_call" | custom-call | tf_op jit(solution)/shard_map/turn1/pallas_call | solution.py:209
  233.4 0.0 copy-start
  233.4 3.0 %copy.6 = f32[2,2,128,1024]{3,2,1,0:T(8,128)} copy(f32[2,2,128,1024]{2,3,0,1:T(8,128)} %bitcast.28) | data formatting | bytes 4194304 | tf_op jit(solution)/shard_map/transpose | solution.py:395
  236.5 0.0 copy-done
  236.5 3.3 %bitcast_add_fusion.1 = f32[4,128,1024]{2,1,0:T(8,128)} fusion(f32[4,128,1024]{2,1,0:T(8,128)S(1)} %copy-done, f32[2,2,128,1024]{3,2,1,0:T(8,128)} %copy.6), kind=kLoop, calls=%fused_computation.4 | loop fusion | flops 524288 | bytes 6291456 | tf_op jit(solution)/shard_map/add | solution.py:400
Async XLA Ops:
  100.7 3.1 %copy-start.1 = (f32[2,2,128,1024]{3,2,1,0:T(8,128)S(1)}, f32[2,2,128,1024]{3,2,1,0:T(8,128)}, u32[]{:S(2)}) copy-start(f32[2,2,128,1024]{3,2,1,0:T(8,128)} %param.4) | copy-start | bytes 6291460
  103.8 3.6 %copy-start.2 = (f32[4,1024,128]{2,1,0:T(8,128)S(1)}, f32[4,1024,128]{2,1,0:T(8,128)}, u32[]{:S(2)}) copy-start(f32[4,1024,128]{2,1,0:T(8,128)} %get-tuple-element.7) | copy-start | bytes 6291460
  103.8 3.6 %copy-start.4 = (f32[4,1024,128]{2,1,0:T(8,128)S(1)}, f32[4,1024,128]{2,1,0:T(8,128)}, u32[]{:S(2)}) copy-start(f32[4,1024,128]{2,1,0:T(8,128)} %get-tuple-element.8) | copy-start | bytes 6291460
  112.5 61.9 %copy-start.3 = (f32[4,128,1024]{2,1,0:T(8,128)S(1)}, f32[4,128,1024]{2,1,0:T(8,128)}, u32[]{:S(2)}) copy-start(f32[4,128,1024]{2,1,0:T(8,128)} %bitcast_add_fusion) | copy-start | bytes 6291460
  233.4 3.1 %copy-start = (f32[4,128,1024]{2,1,0:T(8,128)S(1)}, f32[4,128,1024]{2,1,0:T(8,128)}, u32[]{:S(2)}) copy-start(f32[4,128,1024]{2,1,0:T(8,128)} %fusion.refs_0_) | copy-start | bytes 6291460

commit v4 on v1

v4 whole, which is shorter than its diff:
```python
import functools

import jax
import jax.numpy as jnp
from jax import lax
from jax.experimental import pallas as pl
from jax.experimental.pallas import tpu as pltpu
from jax.sharding import PartitionSpec as P

BLK = 128
MESH = pl.DeviceIdType.MESH
COLORS = ((0, 384), (384, 384), (768, 256))
ORDER = ((0, 2), (1, 2), (0, 1), (0, 3), (1, 1), (1, 3), (1, 0), (0, 0))
RELAYED = 4
PARTS = 2
NT = (((1,), (1,)), ((), ()))


def places():
    return lax.axis_index("oi"), lax.axis_index("oj"), lax.axis_index("vir")


def ring_place(v, dh, dx):
    return ((v // 4 + dh % 2) % 2) * 4 + (v % 4 + dx % 4) % 4


def block(w):
    return pl.ds(pl.multiple_of(w * BLK, BLK), BLK)


def rows8(start, size):
    return pl.ds(pl.multiple_of(start, 8), size)


def split(values):
    top = values.astype(jnp.bfloat16)
    return top, (values - top.astype(jnp.float32)).astype(jnp.bfloat16)


def product(a, b):
    (a1, a2), (b1, b2) = a, b
    dot = functools.partial(lax.dot_general, dimension_numbers=NT, preferred_element_type=jnp.float32)
    return dot(a1, b1) + (dot(a1, b2) + dot(a2, b1))


def remote(source, target, send, recv, peer):
    return pltpu.make_async_remote_copy(
        src_ref=source, dst_ref=target, send_sem=send, recv_sem=recv, device_id=peer, device_id_type=MESH
    )


class Turn:
    def __init__(self, sources, targets, holds, sems):
        self.sources, self.targets, self.holds = sources, targets, holds
        self.send, self.recv, self.hold_recv, self.forward_send, self.own_sem = sems
        self.oi, self.oj, self.v = places()
        self.same = self.oi == self.oj
        self.apart = (self.oi + 2) % 4 == self.oj
        self.cross = self.oi + self.oj == 3

    def greet(self, more):
        oi, oj, v = self.oi, self.oj, self.v
        barrier = pltpu.get_barrier_semaphore()

        def signal(*peers):
            for peer in peers:
                pl.semaphore_signal(barrier, inc=1, device_id=peer, device_id_type=MESH)

        def everyone(a, b):
            return [(a, b, ring_place(v, dh, dx)) for dh, dx in ORDER]

        signal(*more, *everyone(oj, oi)[:-1])

        @pl.when(jnp.logical_not(self.same))
        def _():
            signal((oj, oi, v))

        @pl.when(self.same)
        def _():
            signal(*everyone((oi + 2) % 4, oi), (oi, 3 - oi, v))

        @pl.when(self.apart)
        def _():
            signal(*everyone(oj, oj), (oi, 3 - oi, v))

        @pl.when(self.cross)
        def _():
            signal((oi, oi, v), (oi, (oi + 2) % 4, v))

        kinds = jnp.where(self.same, 16, jnp.where(self.apart, 17, jnp.where(self.cross, 10, 8)))
        pl.semaphore_wait(barrier, kinds + len(more))

    def tile(self, k, w, part):
        pairs = self.sources[k].shape[0] // PARTS
        return self.sources[k].at[pl.ds(part * pairs, pairs), :, block(w)]

    def slot(self, array, frm, part):
        pairs = array.shape[0] // PARTS
        return array.at[pl.ds(part * pairs, pairs), block(frm), :]

    def straight(self, k, w, frm, part):
        return remote(
            self.tile(k, w, part),
            self.slot(self.targets[k], frm, part),
            self.send.at[k, w, part],
            self.recv.at[k, frm, part],
            (self.oj, self.oi, w),
        )

    def detour(self, k, w, part):
        return remote(
            self.tile(k, w, part),
            self.slot(self.holds[k], self.v, part),
            self.send.at[k, w, part],
            self.hold_recv.at[k, self.v, part],
            (self.oj, self.oj, w),
        )

    def forward(self, k, frm, part, last):
        return remote(
            self.slot(self.holds[k], frm, part),
            self.slot((self.targets if last else self.holds)[k], frm, part),
            self.forward_send.at[k, frm, part],
            (self.recv if last else self.hold_recv).at[k, frm, part],
            (self.oi, (self.oi + 2) % 4 if last else 3 - self.oi, self.v),
        )

    def own(self, k):
        return pltpu.make_async_copy(
            self.sources[k].at[:, :, block(self.v)], self.targets[k].at[:, block(self.v), :], self.own_sem.at[k]
        )

    def goal(self, j):
        return ring_place(self.v, *ORDER[j])

    def came(self, j):
        return ring_place(self.v, -ORDER[j][0], -ORDER[j][1])

    def start(self, k, j):
        w = self.goal(j)

        def straight():
            for part in range(PARTS):
                self.straight(k, w, self.v, part).start()

        if j < RELAYED:
            pl.when(jnp.logical_not(self.apart))(straight)

            @pl.when(self.apart)
            def _():
                for part in range(PARTS):
                    self.detour(k, w, part).start()

        elif j < len(ORDER) - 1:
            straight()
        else:
            pl.when(jnp.logical_not(self.same))(straight)
            pl.when(self.same)(lambda: self.own(k).start())

    def relay(self, k, j):
        frm = self.came(j)
        for part in range(PARTS):

            @pl.when(self.same)
            def _():
                self.forward(k, frm, part, False).wait_recv()
                self.forward(k, frm, part, False).start()

            @pl.when(self.cross)
            def _():
                self.forward(k, frm, part, False).wait_recv()
                self.forward(k, frm, part, True).start()

    def arrive(self, k, j):
        frm = self.came(j)

        def wait():
            for part in range(PARTS):
                self.straight(k, frm, frm, part).wait_recv()

        if j < len(ORDER) - 1:
            wait()
        else:
            pl.when(self.same)(lambda: self.own(k).wait())
            pl.when(jnp.logical_not(self.same))(wait)

    def drain(self, k):
        for j in range(len(ORDER)):

            def sent():
                for part in range(PARTS):
                    self.straight(k, self.goal(j), self.v, part).wait_send()

            if j < len(ORDER) - 1:
                sent()
            else:
                pl.when(jnp.logical_not(self.same))(sent)
            if j < RELAYED:

                @pl.when(self.same | self.cross)
                def _():
                    for part in range(PARTS):
                        self.forward(k, self.came(j), part, True).wait_send()


def turn_sems(count):
    return [pltpu.SemaphoreType.DMA((count, 8, PARTS))] * 4 + [pltpu.SemaphoreType.DMA((count,))]


class Reduce:
    def __init__(self, p, d, acc, core_got, got1, got2, sems):
        self.p, self.d, self.acc, self.core_got, self.got1, self.got2 = p, d, acc, core_got, got1, got2
        self.core_sems, self.one_sems, self.plane_sems = sems
        oi, oj, v = places()
        self.core = oi % 2
        self.at = [v % 4, oj, (v // 4) * 2 + oi // 2]

    def device(self, core, at):
        x, y, z = at
        return (z % 2) * 2 + core, y, (z // 2) * 4 + x

    def shifted(self, moves):
        return self.device(self.core, [(p + moves.get(a, 0)) % 4 for a, p in enumerate(self.at)])

    def peers(self):
        found = [self.device(1 - self.core, self.at)]
        for dx in range(4):
            for dy in range(4):
                for dz in range(4):
                    if 0 in (dx, dy, dz) and (dx, dy, dz) != (0, 0, 0):
                        found.append(self.shifted({0: dx, 1: dy, 2: dz}))
        return found

    def columns(self, g):
        return pl.ds(*COLORS[g])

    def swap(self, g, back, here=True):
        sem = self.core_sems.at[back]
        twin = self.device(1 - self.core, self.at)
        if back:
            part = self.d.at[rows8((self.core if here else 1 - self.core) * 512, 512), self.columns(g)]
            return remote(part, part, sem.at[0, g], sem.at[1, g], twin)
        source = self.p.at[rows8((1 - self.core) * 512, 512), self.columns(g)]
        return remote(source, self.core_got.at[:, self.columns(g)], sem.at[0, g], sem.at[1, g], twin)

    def first(self, g, offset=0):
        return (self.at[g] + offset) % 4

    def rest(self, g, d2=0, d3=0):
        return ((self.at[(g + 1) % 3] + d2) % 4) * 4 + (self.at[(g + 2) % 3] + d3) % 4

    def one_axis(self, g, n, back, landed=False):
        sem = self.one_sems.at[back]
        peer = self.shifted({g: n})
        if back:
            place = self.first(g, -n if landed else 0)
            part = self.d.at[rows8(self.core * 512 + place * 128, 128), self.columns(g)]
            return remote(part, part, sem.at[0, g, n], sem.at[1, g, n], peer)
        source = self.acc.at[rows8(self.first(g, n) * 128, 128), self.columns(g)]
        return remote(source, self.got1.at[n - 1, :, self.columns(g)], sem.at[0, g, n], sem.at[1, g, n], peer)

    def plane(self, g, d2, d3, back, landed=False):
        n = d2 * 4 + d3
        sem = self.plane_sems.at[back]
        peer = self.shifted({(g + 1) % 3: d2, (g + 2) % 3: d3})
        if back:
            place = self.rest(g, -d2, -d3) if landed else self.rest(g)
            part = self.d.at[rows8(self.core * 512 + self.first(g) * 128 + place * 8, 8), self.columns(g)]
            return remote(part, part, sem.at[0, g, n], sem.at[1, g, n], peer)
        source = self.acc.at[rows8(self.first(g) * 128 + self.rest(g, d2, d3) * 8, 8), self.columns(g)]
        return remote(source, self.got2.at[n, :, self.columns(g)], sem.at[0, g, n], sem.at[1, g, n], peer)


AXIS = (2, 1, 3)
PLANE = sorted(((a, b) for a in range(4) for b in range(4) if a or b), key=lambda m: -sum((0, 1, 2, 1)[n] for n in m))
SWAP = (0, 2, 1, 3)


def kernel(
    x_ref, g_ref, fock_ref, kept_ref, out_ref,
    xm, xt, gt, xhold, ghold, z_ref, zt, zhold,
    g_top, g_rest, y_top, y_rest, p_ref, d_ref, acc, core_got, got1, got2,
    *sems,
):
    early = Turn([g_ref, xm], [gt, xt], [ghold, xhold], sems[:5])
    late = Turn([z_ref], [zt], [zhold], sems[5:10])
    reduce = Reduce(p_ref, d_ref, acc, core_got, got1, got2, sems[10:])
    oi, oj, v = places()
    core, half, x = oi % 2, v // 4, v % 4
    early.greet(reduce.peers())

    for j in range(8):
        early.start(0, j)
    for t in range(8):
        keep = kept_ref[v, t].astype(jnp.float32)
        columns = slice(t * BLK, t * BLK + BLK)
        xm[:, :, columns] = x_ref[:, :, columns] * keep
    for j in range(8):
        early.start(1, j)

    def halves(source, w):
        tile = source[:, block(w), :]
        return split(jnp.concatenate([tile[n] for n in range(4)], axis=1))

    for k in range(2):
        for j in range(RELAYED):
            early.relay(k, j)
    for j in range(8):
        early.arrive(0, j)
        w = early.came(j)
        g_top[block(w), :], g_rest[block(w), :] = halves(gt, w)
    for j in range(8):
        early.arrive(1, j)
        w = early.came(j)
        p_ref[block(w), :] = product(halves(xt, w), (g_top[...], g_rest[...]))

    def mixed(t):
        columns = slice(t * BLK, t * BLK + BLK)
        for n in range(4):
            both = xm[n, :, columns] + xt[SWAP[n], columns, :].T
            y_top[n * BLK : n * BLK + BLK, columns], y_rest[n * BLK : n * BLK + BLK, columns] = split(both)

    colours = range(3)
    for g in colours:
        reduce.swap(g, 0).start()
    mixed(0)
    for g in colours:
        at = reduce.columns(g)
        reduce.swap(g, 0).wait_recv()
        acc[:, at] = p_ref[rows8(core * 512, 512), at] + core_got[:, at]

        @pl.when((oj == 0) & (oi == half))
        def _():
            acc[block(x), at] -= fock_ref[:, at]

        for n in AXIS:
            reduce.one_axis(g, n, 0).start()
    mixed(1)
    mixed(2)
    mixed(3)
    for g in colours:
        at = reduce.columns(g)
        for n in AXIS:
            reduce.one_axis(g, n, 0).wait_recv()
        here = block(reduce.first(g))
        acc[here, at] = (acc[here, at] + got1[0, :, at]) + (got1[1, :, at] + got1[2, :, at])
        for move in PLANE:
            reduce.plane(g, *move, 0).start()
    mixed(4)
    mixed(5)
    for g in colours:
        at = reduce.columns(g)
        mine = reduce.first(g) * 128 + reduce.rest(g) * 8
        total = acc[rows8(mine, 8), at]
        for move in PLANE:
            reduce.plane(g, *move, 0).wait_recv()
            total = total + got2[move[0] * 4 + move[1], :, at]
        d_ref[rows8(core * 512 + mine, 8), at] = -total
        for move in PLANE:
            reduce.plane(g, *move, 1).start()
    mixed(6)
    mixed(7)
    for g in colours:
        for move in PLANE:
            reduce.plane(g, *move, 1, True).wait_recv()
        for n in AXIS:
            reduce.one_axis(g, n, 1).start()
    for g in colours:
        for n in AXIS:
            reduce.one_axis(g, n, 1, True).wait_recv()
        reduce.swap(g, 1).start()
    for g in colours:
        reduce.swap(g, 1, False).wait_recv()

    for j in range(0, 8, 2):
        ws = [late.goal(j), late.goal(j + 1)]
        d_rows = jnp.concatenate([d_ref[block(w), :] for w in ws], axis=0)
        part = product((y_top[...], y_rest[...]), split(d_rows))
        for m, w in enumerate(ws):
            for n in range(4):
                z_ref[n, :, block(w)] = part[n * BLK : n * BLK + BLK, m * BLK : m * BLK + BLK]
            late.start(0, j + m)
        if j >= 4:
            late.relay(0, j - 4)
            late.relay(0, j - 3)
    for j in range(8):
        late.arrive(0, j)
        w = late.came(j)
        for n in range(4):
            out_ref[n, :, block(w)] = z_ref[n, :, block(w)] + zt[SWAP[n], block(w), :].T

    early.drain(0)
    early.drain(1)
    late.drain(0)
    for back in range(2):
        for g in colours:
            reduce.swap(g, back).wait_send()
            for n in AXIS:
                reduce.one_axis(g, n, back).wait_send()
            for move in PLANE:
                reduce.plane(g, *move, back).wait_send()


def body(amplitudes, integrals, fock_virtual, screening):
    shape = amplitudes.shape
    rows, width = shape[2:]
    pairs = shape[0] * shape[1]
    f32, bf16 = jnp.float32, jnp.bfloat16
    vmem = pl.BlockSpec(memory_space=pltpu.VMEM)
    lying, standing = pltpu.VMEM((pairs, rows, width), f32), pltpu.VMEM((pairs, width, rows), f32)
    dma = pltpu.SemaphoreType.DMA
    out = pl.pallas_call(
        kernel,
        out_shape=jax.ShapeDtypeStruct((pairs, rows, width), f32),
        in_specs=[vmem] * 3 + [pl.BlockSpec(memory_space=pltpu.SMEM)],
        out_specs=vmem,
        scratch_shapes=[lying]
        + [standing] * 4
        + [lying]
        + [standing] * 2
        + [pltpu.VMEM((width, pairs * rows), bf16)] * 2
        + [pltpu.VMEM((pairs * rows, width), bf16)] * 2
        + [pltpu.VMEM((width, width), f32)] * 2
        + [pltpu.VMEM((width // 2, width), f32)] * 2
        + [pltpu.VMEM((3, 128, width), f32), pltpu.VMEM((16, 8, width), f32)]
        + turn_sems(2)
        + turn_sems(1)
        + [dma((2, 2, 3)), dma((2, 2, 3, 4)), dma((2, 2, 3, 16))],
        compiler_params=pltpu.CompilerParams(collective_id=1, has_side_effects=True, vmem_limit_bytes=60 * 2**20),
        name="residual",
    )(
        amplitudes.reshape(pairs, rows, width),
        integrals.reshape(pairs, rows, width),
        fock_virtual,
        screening.reshape(screening.shape[2:]),
    )
    return out.reshape(shape)


def solution(mesh):
    placed = (
        P("oi", "oj", "vir", None),
        P("oi", "oj", "vir", None),
        P("vir", None),
        P("oi", "oj", None, None),
    )
    return jax.shard_map(
        body, mesh=mesh, in_specs=placed, out_specs=P("oi", "oj", "vir", None), check_vma=False
    )
```

time: 1250 us -> 185 us (0.15)
  waiting for transfers between devices: 1140 us -> 0 us
  Pallas kernels: 0 us -> 178 us
  blocking collectives: 35.8 us -> 0 us
  starting transfers between devices: 23.5 us -> 0 us
  local copies, waits for them, and re-layouts: 25.4 us -> 3.16 us
  matrix products: 15.5 us -> 0 us
  between operations: 13.5 us -> 0.01 us
    reduce_scatter x1 -> x0, waiting for transfers between devices: 638 us -> none  [body(): lax.psum_scatter(partial, ('vir', 'oi', 'oj'), scatter_dimension=0, tiled...]
    all_gather x1 -> x0, waiting for transfers between devices: 310 us -> none  [body(): lax.all_gather(mine - share, ('vir', 'oi', 'oj'), axis=0, tiled=True)]
    pallas_call x0 -> x1, Pallas kernels: none -> 178 us  [body(): pl.pallas_call(kernel, out_shape=jax.ShapeDtypeStruct((pairs, rows, width...]
    ppermute x3 -> x0, waiting for transfers between devices: 139 us -> none  [turn(): return lax.ppermute(sent, ('oi', 'oj'), mirror_perm(n))]
    all_to_all x2 -> x0, waiting for transfers between devices: 48.9 us -> none  [turn(): lax.all_to_all(swapped, 'vir', split_axis=3, concat_axis=2, tiled=True)]
    all_to_all x1 -> x0, blocking collectives: 35.8 us -> none  [turn(): lax.all_to_all(swapped, 'vir', split_axis=3, concat_axis=2, tiled=True)]
    dot_general x2 -> x0, matrix products: 15.5 us -> none  [the longest x1 10.3 us: body(): jnp.einsum('pac,bc->pab', both.reshape(pairs, rows_here, width), dressed,...]
    all_to_all x2 -> x0, starting transfers between devices: 13.7 us -> none  [turn(): lax.all_to_all(swapped, 'vir', split_axis=3, concat_axis=2, tiled=True)]
  transfers between devices with their start and end apart: 7 -> 0, of which waited for: 7 -> 0; matrix products, arithmetic and copies ran while one was open for 1% -> 0% of each run, Pallas kernels for 0% -> 0%
where the time goes in v4:
time: 185 us; the launch traced here: 181 us
  Pallas kernels  178 us (96%)
  local copies, waits for them, and re-layouts  3.16 us (2%)
    pallas_call x1, Pallas kernels, body(): pl.pallas_call(kernel, out_shape=jax.ShapeDtypeStruct((pairs, rows, width...  178 us

profile of v4, /device:TPU:24, one launch (start us, length us, event | category | flops | bytes accessed | tf_op | source)
XLA Modules:
  0.0 181.4 jit_solution(2884689902530757316)
XLA Ops:
  0.0 178.2 %residual.1 = f32[4,128,1024]{2,1,0:T(8,128)} custom-call(f32[4,128,1024]{2,1,0:T(8,128)} %bitcast.5, f32[4,128,1024]{2,1,0:T(8,128)} %bitcast.6, f32[128,1024]{1,0:T(8,128)} %fock_ref.1, s32[8,8]{1,0:T(8,128)} %bitcast.7), custom_call_target="tpu_custom_call" | custom-call | tf_op jit(solution)/shard_map/residual/pallas_call | solution.py:412
  178.2 3.2 %copy.6 = f32[2,2,128,1024]{3,2,1,0:T(8,128)} copy(f32[2,2,128,1024]{3,2,1,0:T(8,128)} %bitcast.4) | data formatting | bytes 4194304

commit v5 on v4

--- a/solution.py
+++ b/solution.py
@@ -9,10 +9,10 @@
 
 BLK = 128
 MESH = pl.DeviceIdType.MESH
-COLORS = ((0, 384), (384, 384), (768, 256))
+COLORS = ((0, 256), (256, 256), (512, 256), (768, 128), (896, 128))
 ORDER = ((0, 2), (1, 2), (0, 1), (0, 3), (1, 1), (1, 3), (1, 0), (0, 0))
 RELAYED = 4
-PARTS = 2
+PARTS = 1
 NT = (((1,), (1,)), ((), ()))
 
 
@@ -210,7 +210,7 @@
 class Reduce:
     def __init__(self, p, d, acc, core_got, got1, got2, sems):
         self.p, self.d, self.acc, self.core_got, self.got1, self.got2 = p, d, acc, core_got, got1, got2
-        self.core_sems, self.one_sems, self.plane_sems = sems
+        self.give_sems, self.back_sems, self.one_sems, self.plane_sems = sems
         oi, oj, v = places()
         self.core = oi % 2
         self.at = [v % 4, oj, (v // 4) * 2 + oi // 2]
@@ -234,24 +234,42 @@
     def columns(self, g):
         return pl.ds(*COLORS[g])
 
-    def swap(self, g, back, here=True):
-        sem = self.core_sems.at[back]
+    def give(self, w):
+        q = w % 4
         twin = self.device(1 - self.core, self.at)
-        if back:
-            part = self.d.at[rows8((self.core if here else 1 - self.core) * 512, 512), self.columns(g)]
-            return remote(part, part, sem.at[0, g], sem.at[1, g], twin)
-        source = self.p.at[rows8((1 - self.core) * 512, 512), self.columns(g)]
-        return remote(source, self.core_got.at[:, self.columns(g)], sem.at[0, g], sem.at[1, g], twin)
+        return remote(self.p.at[block(w)], self.core_got.at[block(q)], self.give_sems.at[0, q], self.give_sems.at[1, q], twin)
+
+    def give_back(self, g, q, here=True):
+        half = self.core if here else 1 - self.core
+        part = self.d.at[block(half * 4 + q), self.columns(g)]
+        sems = self.back_sems
+        return remote(part, part, sems.at[0, g, q], sems.at[1, g, q], self.device(1 - self.core, self.at))
+
+    def send_block(self, g, q):
+        n = (q + 4 - self.at[g % 3]) % 4
+        sems = self.one_sems.at[0]
+        at = list(self.at)
+        at[g % 3] = q
+
+        @pl.when(n != 0)
+        def _():
+            remote(
+                self.acc.at[block(q), self.columns(g)],
+                self.got1.at[n - 1, :, self.columns(g)],
+                sems.at[0, g, n],
+                sems.at[1, g, n],
+                self.device(self.core, at),
+            ).start()
 
     def first(self, g, offset=0):
-        return (self.at[g] + offset) % 4
+        return (self.at[g % 3] + offset) % 4
 
     def rest(self, g, d2=0, d3=0):
         return ((self.at[(g + 1) % 3] + d2) % 4) * 4 + (self.at[(g + 2) % 3] + d3) % 4
 
     def one_axis(self, g, n, back, landed=False):
         sem = self.one_sems.at[back]
-        peer = self.shifted({g: n})
+        peer = self.shifted({g % 3: n})
         if back:
             place = self.first(g, -n if landed else 0)
             part = self.d.at[rows8(self.core * 512 + place * 128, 128), self.columns(g)]
@@ -277,8 +295,8 @@
 
 
 def kernel(
-    x_ref, g_ref, fock_ref, kept_ref, out_ref,
-    xm, xt, gt, xhold, ghold, z_ref, zt, zhold,
+    x_far, g_ref, fock_far, kept_ref, out_far,
+    out_ref, store_sem, x_ref, fock_ref, load_sem, xm, xt, gt, xhold, ghold, z_ref, zt, zhold,
     g_top, g_rest, y_top, y_rest, p_ref, d_ref, acc, core_got, got1, got2,
     *sems,
 ):
@@ -286,11 +304,19 @@
     late = Turn([z_ref], [zt], [zhold], sems[5:10])
     reduce = Reduce(p_ref, d_ref, acc, core_got, got1, got2, sems[10:])
     oi, oj, v = places()
-    core, half, x = oi % 2, v // 4, v % 4
+    core, half = oi % 2, v // 4
+    loads = [
+        pltpu.make_async_copy(x_far, x_ref, load_sem.at[0]),
+        pltpu.make_async_copy(fock_far, fock_ref, load_sem.at[1]),
+    ]
+    for load in loads:
+        load.start()
     early.greet(reduce.peers())
 
     for j in range(8):
         early.start(0, j)
+    for load in loads:
+        load.wait()
     for t in range(8):
         keep = kept_ref[v, t].astype(jnp.float32)
         columns = slice(t * BLK, t * BLK + BLK)
@@ -309,10 +335,31 @@
         early.arrive(0, j)
         w = early.came(j)
         g_top[block(w), :], g_rest[block(w), :] = halves(gt, w)
+
+    def take(j):
+        w = early.came(j)
+        q = w % 4
+
+        @pl.when(w // 4 == core)
+        def _():
+            reduce.give(w).wait_recv()
+            acc[block(q), :] = p_ref[block(w), :] + core_got[block(q), :]
+            if j == 7:
+
+                @pl.when((oj == 0) & (oi == half))
+                def _():
+                    acc[block(q), :] -= fock_ref[...]
+
+            for g in range(len(COLORS)):
+                reduce.send_block(g, q)
+
     for j in range(8):
         early.arrive(1, j)
         w = early.came(j)
         p_ref[block(w), :] = product(halves(xt, w), (g_top[...], g_rest[...]))
+        pl.when(w // 4 != core)(lambda: reduce.give(w).start())
+        if j:
+            take(j - 1)
 
     def mixed(t):
         columns = slice(t * BLK, t * BLK + BLK)
@@ -320,21 +367,9 @@
             both = xm[n, :, columns] + xt[SWAP[n], columns, :].T
             y_top[n * BLK : n * BLK + BLK, columns], y_rest[n * BLK : n * BLK + BLK, columns] = split(both)
 
-    colours = range(3)
-    for g in colours:
-        reduce.swap(g, 0).start()
+    colours = range(len(COLORS))
     mixed(0)
-    for g in colours:
-        at = reduce.columns(g)
-        reduce.swap(g, 0).wait_recv()
-        acc[:, at] = p_ref[rows8(core * 512, 512), at] + core_got[:, at]
-
-        @pl.when((oj == 0) & (oi == half))
-        def _():
-            acc[block(x), at] -= fock_ref[:, at]
-
-        for n in AXIS:
-            reduce.one_axis(g, n, 0).start()
+    take(7)
     mixed(1)
     mixed(2)
     mixed(3)
@@ -365,12 +400,14 @@
             reduce.plane(g, *move, 1, True).wait_recv()
         for n in AXIS:
             reduce.one_axis(g, n, 1).start()
+        reduce.give_back(g, reduce.first(g)).start()
+    for n in (1, 3, 2):
+        for g in colours:
+            reduce.one_axis(g, n, 1, True).wait_recv()
+            reduce.give_back(g, reduce.first(g, -n)).start()
     for g in colours:
-        for n in AXIS:
-            reduce.one_axis(g, n, 1, True).wait_recv()
-        reduce.swap(g, 1).start()
-    for g in colours:
-        reduce.swap(g, 1, False).wait_recv()
+        for q in range(4):
+            reduce.give_back(g, q, False).wait_recv()
 
     for j in range(0, 8, 2):
         ws = [late.goal(j), late.goal(j + 1)]
@@ -388,13 +425,20 @@
         w = late.came(j)
         for n in range(4):
             out_ref[n, :, block(w)] = z_ref[n, :, block(w)] + zt[SWAP[n], block(w), :].T
+        pltpu.make_async_copy(out_ref.at[:, :, block(w)], out_far.at[:, :, block(w)], store_sem.at[j]).start()
 
     early.drain(0)
     early.drain(1)
     late.drain(0)
+    for j in range(8):
+        w = late.came(j)
+        pltpu.make_async_copy(out_ref.at[:, :, block(w)], out_far.at[:, :, block(w)], store_sem.at[j]).wait()
+    for q in range(4):
+        reduce.give(q).wait_send()
+        for g in colours:
+            reduce.give_back(g, q).wait_send()
     for back in range(2):
         for g in colours:
-            reduce.swap(g, back).wait_send()
             for n in AXIS:
                 reduce.one_axis(g, n, back).wait_send()
             for move in PLANE:
@@ -406,15 +450,14 @@
     rows, width = shape[2:]
     pairs = shape[0] * shape[1]
     f32, bf16 = jnp.float32, jnp.bfloat16
-    vmem = pl.BlockSpec(memory_space=pltpu.VMEM)
     lying, standing = pltpu.VMEM((pairs, rows, width), f32), pltpu.VMEM((pairs, width, rows), f32)
     dma = pltpu.SemaphoreType.DMA
     out = pl.pallas_call(
         kernel,
         out_shape=jax.ShapeDtypeStruct((pairs, rows, width), f32),
-        in_specs=[vmem] * 3 + [pl.BlockSpec(memory_space=pltpu.SMEM)],
-        out_specs=vmem,
-        scratch_shapes=[lying]
+        in_specs=[pl.BlockSpec(memory_space=pl.ANY)] * 3 + [pl.BlockSpec(memory_space=pltpu.SMEM)],
+        out_specs=pl.BlockSpec(memory_space=pl.ANY),
+        scratch_shapes=[lying, dma((8,)), lying, pltpu.VMEM((rows, width), f32), dma((2,)), lying]
         + [standing] * 4
         + [lying]
         + [standing] * 2
@@ -425,7 +468,8 @@
         + [pltpu.VMEM((3, 128, width), f32), pltpu.VMEM((16, 8, width), f32)]
         + turn_sems(2)
         + turn_sems(1)
-        + [dma((2, 2, 3)), dma((2, 2, 3, 4)), dma((2, 2, 3, 16))],
+        + [dma((2, 4))]
+        + [dma((2, len(COLORS), 4)), dma((2, 2, len(COLORS), 4)), dma((2, 2, len(COLORS), 16))],
         compiler_params=pltpu.CompilerParams(collective_id=1, has_side_effects=True, vmem_limit_bytes=60 * 2**20),
         name="residual",
     )(

time: 185 us -> 179 us (0.968)
  Pallas kernels: 178 us -> 173 us
    pallas_call x1, Pallas kernels: 178 us -> 173 us  [body(): pl.pallas_call(kernel, out_shape=jax.ShapeDtypeStruct((pairs, rows, width...]
where the time goes in v5:
time: 179 us; the launch traced here: 176 us
  Pallas kernels  173 us (97%)
  local copies, waits for them, and re-layouts  3.16 us (2%)
    pallas_call x1, Pallas kernels, body(): pl.pallas_call(kernel, out_shape=jax.ShapeDtypeStruct((pairs, rows, width...  173 us

profile of v5, /device:TPU:24, one launch (start us, length us, event | category | flops | bytes accessed | tf_op | source)
XLA Modules:
  0.0 176.1 jit_solution(13550059905697912701)
XLA Ops:
  0.0 173.0 %residual.1 = f32[4,128,1024]{2,1,0:T(8,128)} custom-call(f32[4,128,1024]{2,1,0:T(8,128)} %bitcast.5, f32[4,128,1024]{2,1,0:T(8,128)} %bitcast.6, f32[128,1024]{1,0:T(8,128)} %fock_far.1, s32[8,8]{1,0:T(8,128)} %bitcast.7), custom_call_target="tpu_custom_call" | custom-call | tf_op jit(solution)/shard_map/residual/pallas_call | solution.py:455
  173.0 3.2 %copy.6 = f32[2,2,128,1024]{3,2,1,0:T(8,128)} copy(f32[2,2,128,1024]{3,2,1,0:T(8,128)} %bitcast.4) | data formatting | bytes 4194304

commit v6 on v5

--- a/solution.py
+++ b/solution.py
@@ -417,9 +417,12 @@
             for n in range(4):
                 z_ref[n, :, block(w)] = part[n * BLK : n * BLK + BLK, m * BLK : m * BLK + BLK]
             late.start(0, j + m)
-        if j >= 4:
-            late.relay(0, j - 4)
-            late.relay(0, j - 3)
+        if j == 2:
+            late.relay(0, 0)
+        if j == 4:
+            late.relay(0, 1)
+    late.relay(0, 2)
+    late.relay(0, 3)
     for j in range(8):
         late.arrive(0, j)
         w = late.came(j)

time: 179 us -> 179 us (level)
  no operation moved by 1% of the time
where the time goes in v6:
time: 179 us; the launch traced here: 176 us
  Pallas kernels  173 us (97%)
  local copies, waits for them, and re-layouts  3.16 us (2%)
    pallas_call x1, Pallas kernels, body(): pl.pallas_call(kernel, out_shape=jax.ShapeDtypeStruct((pairs, rows, width...  173 us

profile of v6, /device:TPU:24, one launch (start us, length us, event | category | flops | bytes accessed | tf_op | source)
XLA Modules:
  0.0 176.1 jit_solution(106849793406629553)
XLA Ops:
  0.0 173.0 %residual.1 = f32[4,128,1024]{2,1,0:T(8,128)} custom-call(f32[4,128,1024]{2,1,0:T(8,128)} %bitcast.5, f32[4,128,1024]{2,1,0:T(8,128)} %bitcast.6, f32[128,1024]{1,0:T(8,128)} %fock_far.1, s32[8,8]{1,0:T(8,128)} %bitcast.7), custom_call_target="tpu_custom_call" | custom-call | tf_op jit(solution)/shard_map/residual/pallas_call | solution.py:458
  173.0 3.2 %copy.6 = f32[2,2,128,1024]{3,2,1,0:T(8,128)} copy(f32[2,2,128,1024]{3,2,1,0:T(8,128)} %bitcast.4) | data formatting | bytes 4194304
